TPU v7x, 32 devices: a whole 2x2x4 slice. The times are simulated.
32 devices in a mesh: pair: 8 (over z, x), row: 4 (over y, core).
Axes of the slice: x: 2, y: 2, z: 4, core: 2. Of those that a mesh axis runs over, the one named last changes fastest.
Arguments:
- records: bfloat16 [128, 4096, 8], P('row', 'pair'), may hold values from -10 to 10
- offsets: float32 [8, 128], P('pair', 'row'), may hold values from -1 to 1
- counts: int32 [8], replicated, may hold values from 64 to 128, as said below
- damping: float32 [1], replicated, may hold values from 0.1 to 1
Outputs:
- offset_step: float32 [8, 128], P('pair', 'row')
Inputs may be any that keep to these rules, and one draw needn't show every extreme that they name: Channel i of block b is live when i < counts[b]; in every draw some block has all 128 channels live.
All inputs are finite; a program needn't handle non-finite values.
Results may differ from a plain program's by a relative error of at most 0.0044.
Values may be sent and summed in bfloat16 or wider, within the bound.
No kernel may reach another device: no remote copies, remote signals or barrier semaphores. Data moves between devices by JAX's collectives and lax.ppermute only.
A program may use at most 64 MiB of HBM per device.

v0:
```python
import math
import jax
import jax.numpy as jnp
from jax import lax
from jax.sharding import PartitionSpec as P

CB = 128
NF = 512
NLAG = 256


def band_table(row_start, row_count, samples, first_bin, freq_count):
    sample_ids = row_start + jnp.arange(row_count, dtype=jnp.int32)
    freq_bins = first_bin + jnp.arange(freq_count, dtype=jnp.int32)
    phase_ids = sample_ids[:, None] * freq_bins[None, :] % samples
    angles = phase_ids.astype(jnp.float32) * (2.0 * math.pi / samples)
    return jnp.concatenate([jnp.cos(angles), jnp.sin(angles)], axis=1)


def lag_weights(samples, first_bin, freq_count, lag_count):
    freq_bins = first_bin + jnp.arange(freq_count, dtype=jnp.int32)
    lag_ids = 1 + jnp.arange(lag_count, dtype=jnp.int32)
    phase_ids = freq_bins[:, None] * lag_ids[None, :] % samples
    angles = phase_ids.astype(jnp.float32) * (2.0 * math.pi / samples)
    centre = (jnp.arange(freq_count, dtype=jnp.float32) + 0.5) * (math.pi / freq_count)
    weight = jnp.sin(centre) ** 2
    return (-2.0 * weight[:, None] * jnp.sin(angles)).astype(jnp.bfloat16)


def pair_stats(own_spec, partners, lag_table, angular):
    own_re = own_spec[:, 0].astype(jnp.float32)
    own_im = own_spec[:, 1].astype(jnp.float32)
    far_re = partners[:, :, 0].astype(jnp.float32)
    far_im = partners[:, :, 1].astype(jnp.float32)
    cross_re = own_re * far_re + own_im * far_im
    cross_im = own_im * far_re - own_re * far_im
    stacked = jnp.stack([cross_im, angular * cross_re]).astype(jnp.bfloat16)
    lagged = jnp.dot(stacked, lag_table, preferred_element_type=jnp.float32)
    residual = lagged[0]
    jacobian = lagged[1]
    return (jnp.sum(jacobian * jacobian, axis=-1), jnp.sum(jacobian * residual, axis=-1))


def per_device(records, offsets, counts, damping):
    nblock = lax.axis_size("pair")
    block_rank = lax.axis_index("pair")
    quarter = lax.axis_index("row")
    relaid = lax.all_to_all(records, "pair", split_axis=2, concat_axis=1, tiled=True)
    signal = relaid[:, :, 0]
    channels = signal.shape[0]
    samples = signal.shape[1]
    first_bin = samples // 8
    block_len = samples // 8

    def accumulate(partial_value, turn_index):
        first_row = turn_index * block_len
        segment = lax.dynamic_slice_in_dim(signal, first_row, block_len, 1)
        dft_table = band_table(first_row, block_len, samples, first_bin, NF)
        table_high = dft_table.astype(jnp.bfloat16)
        table_low = (dft_table - table_high.astype(jnp.float32)).astype(jnp.bfloat16)
        partial_value = partial_value + jnp.dot(
            segment, table_high, preferred_element_type=jnp.float32
        )
        partial_value = partial_value + jnp.dot(
            segment, table_low, preferred_element_type=jnp.float32
        )
        return (partial_value, None)

    spectrum, _ = lax.scan(
        accumulate, jnp.zeros((channels, 2 * NF), jnp.float32), jnp.arange(8, dtype=jnp.int32)
    )
    cosine_part = spectrum[:, :NF]
    sine_part = spectrum[:, NF:]
    angular = (first_bin + jnp.arange(NF, dtype=jnp.int32)).astype(jnp.float32) * (
        2.0 * math.pi / samples
    )
    shift_angle = offsets[0][:, None] * angular[None, :]
    shift_cos = jnp.cos(shift_angle)
    shift_sin = jnp.sin(shift_angle)
    real_part = cosine_part * shift_cos + sine_part * shift_sin
    imag_part = cosine_part * shift_sin - sine_part * shift_cos
    live_count = lax.dynamic_index_in_dim(counts, block_rank, keepdims=False)
    channel_ids = quarter * channels + jnp.arange(channels, dtype=jnp.int32)
    alive = (channel_ids < live_count).astype(jnp.float32)
    energy = jnp.mean(real_part * real_part + imag_part * imag_part, axis=1)
    weight_scale = alive / jnp.sqrt(energy + 1e-06)
    own_spec = jnp.stack(
        [real_part * weight_scale[:, None], imag_part * weight_scale[:, None]], axis=1
    ).astype(jnp.bfloat16)
    lag_table = lag_weights(samples, first_bin, NF, NLAG)
    segment = lax.all_gather(own_spec[None], "pair", axis=0, tiled=True)
    squares_part, products_part = pair_stats(own_spec, segment, lag_table, angular)
    partner_ids = jnp.arange(segment.shape[0], dtype=jnp.int32)
    keep_mask = (partner_ids > block_rank).astype(jnp.float32)[:, None]
    new_squares = squares_part * keep_mask
    new_products = products_part * keep_mask
    eye_blocks = jnp.eye(nblock, dtype=jnp.float32)
    onehot = (jnp.arange(nblock, dtype=jnp.int32) == block_rank).astype(jnp.float32)
    sq_t = new_squares.T
    pr_t = new_products.T
    crossing = sq_t[:, None, :] * onehot[None, :, None]
    diag_vals = sq_t + onehot[None, :] * jnp.sum(sq_t, axis=1, keepdims=True)
    hessian = diag_vals[:, :, None] * eye_blocks[None] - crossing - jnp.swapaxes(crossing, 1, 2)
    gradient = onehot[None, :] * jnp.sum(pr_t, axis=1, keepdims=True) - pr_t
    hessian, gradient = lax.psum((hessian, gradient), "pair")
    diagonal = jnp.diagonal(hessian, axis1=1, axis2=2)
    trace_sum = lax.psum(jnp.sum(diagonal), "row")
    level_mean = trace_sum / (nblock * CB)
    damped = damping[0] * (diagonal + level_mean)
    system = hessian + damped[:, :, None] * eye_blocks[None]
    factor = jnp.linalg.cholesky(system)
    update = -jax.scipy.linalg.cho_solve((factor, True), gradient[:, :, None])[:, :, 0]
    return lax.dynamic_slice_in_dim(update, block_rank, 1, 1).T


def solution(mesh):
    return jax.shard_map(
        per_device,
        mesh=mesh,
        in_specs=(P("row", "pair", None), P("pair", "row"), P(), P()),
        out_specs=P("pair", "row"),
        check_vma=False,
    )
```

profile of v0, /device:TPU:0, one launch (start us, length us, event | category | flops | bytes accessed | tf_op | source)
XLA Modules:
  0.0 172.0 jit_solution(3710374380044799579)
XLA Ops:
  0.0 1.7 %copy.35 = bf16[32,512,8]{1,0,2:T(8,128)(2,1)} copy(bf16[32,512,8]{1,2,0:T(8,128)(2,1)} %param.6) | data formatting | bytes 524288 | tf_op args[0]
  1.7 7.3 %all-to-all-start = ((bf16[32,512,8]{1,0,2:T(8,128)(2,1)}), bf16[32,512,8]{1,0,2:T(8,128)(2,1)S(1)}, u32[]{:S(2)}, u32[]{:S(2)}) async-start(bf16[32,512,8]{1,0,2:T(8,128)(2,1)} %copy.35), calls=%async_computation | async-start | bytes 524288 | tf_op jit(solution)/shard_map/all_to_all | solution.py:48
  9.2 0.6 dynamic_slice.20
  9.9 8.1 %all-to-all-done = bf16[32,512,8]{1,0,2:T(8,128)(2,1)S(1)} async-done(((bf16[32,512,8]{1,0,2:T(8,128)(2,1)}), bf16[32,512,8]{1,0,2:T(8,128)(2,1)S(1)}, u32[]{:S(2)}, u32[]{:S(2)}) %all-to-all-start) | async-done | bytes 262176 | tf_op jit(solution)/shard_map/all_to_all | solution.py:48
  18.0 48.9 %while.13 = (s32[]{:T(128)}, f32[32,1024]{1,0:T(8,128)S(1)}, s32[8]{0:T(128)S(1)}, bf16[32,4096]{1,0:T(8,128)(2,1)S(1)}, s32[]{:T(128)}, /*index=5*/s32[1]{0:T(128)}, s32[]{:T(128)}, s32[]{:T(128)}) while((s32[]{:T(128)}, f32[32,1024]{1,0:T(8,128)S(1)}, s32[8]{0:T(128)S(1)}, bf16[32,4096]{1,0:T(8,128)(2,1)S(1)}, s32[]{:T(128)}, ...), condition=%wide.region_1.2_spmd.clone, body=%wide.region_0.1_spmd.clone.sunk | while | flops 75596808 | bytes 6889645 | solution.py:69
  18.0 0.7 dynamic_slice.34
  19.4 4.1 %fusion.70 = (f32[512,512]{1,0:T(8,128)S(1)}, f32[512,512]{1,0:T(8,128)S(1)}) fusion(s32[512]{0:T(512)S(1)} %get-tuple-element.138, s32[512]{0:T(512)S(1)} %get-tuple-element.139), kind=kLoop, calls=%fused_computation.16.clone.1 | loop fusion | flops 3670016 | bytes 2101248 | tf_op jit(solution)/shard_map/while/body/eval_jaxpr/cos | solution.py:17
  23.5 0.3 fusion.71
  23.8 0.3 convolution_add_fusion.2
  24.1 0.7 dynamic_slice.34
  25.5 4.1 %fusion.70 = (f32[512,512]{1,0:T(8,128)S(1)}, f32[512,512]{1,0:T(8,128)S(1)}) fusion(s32[512]{0:T(512)S(1)} %get-tuple-element.138, s32[512]{0:T(512)S(1)} %get-tuple-element.139), kind=kLoop, calls=%fused_computation.16.clone.1 | loop fusion | flops 3670016 | bytes 2101248 | tf_op jit(solution)/shard_map/while/body/eval_jaxpr/cos | solution.py:17
  29.6 0.3 fusion.71
  29.9 0.3 convolution_add_fusion.2
  30.2 0.7 dynamic_slice.34
  31.6 4.1 %fusion.70 = (f32[512,512]{1,0:T(8,128)S(1)}, f32[512,512]{1,0:T(8,128)S(1)}) fusion(s32[512]{0:T(512)S(1)} %get-tuple-element.138, s32[512]{0:T(512)S(1)} %get-tuple-element.139), kind=kLoop, calls=%fused_computation.16.clone.1 | loop fusion | flops 3670016 | bytes 2101248 | tf_op jit(solution)/shard_map/while/body/eval_jaxpr/cos | solution.py:17
  35.8 0.3 fusion.71
  36.1 0.3 convolution_add_fusion.2
  36.3 0.7 dynamic_slice.34
  37.7 4.1 %fusion.70 = (f32[512,512]{1,0:T(8,128)S(1)}, f32[512,512]{1,0:T(8,128)S(1)}) fusion(s32[512]{0:T(512)S(1)} %get-tuple-element.138, s32[512]{0:T(512)S(1)} %get-tuple-element.139), kind=kLoop, calls=%fused_computation.16.clone.1 | loop fusion | flops 3670016 | bytes 2101248 | tf_op jit(solution)/shard_map/while/body/eval_jaxpr/cos | solution.py:17
  41.9 0.3 fusion.71
  42.2 0.3 convolution_add_fusion.2
  42.5 0.7 dynamic_slice.34
  43.8 4.1 %fusion.70 = (f32[512,512]{1,0:T(8,128)S(1)}, f32[512,512]{1,0:T(8,128)S(1)}) fusion(s32[512]{0:T(512)S(1)} %get-tuple-element.138, s32[512]{0:T(512)S(1)} %get-tuple-element.139), kind=kLoop, calls=%fused_computation.16.clone.1 | loop fusion | flops 3670016 | bytes 2101248 | tf_op jit(solution)/shard_map/while/body/eval_jaxpr/cos | solution.py:17
  48.0 0.3 fusion.71
  48.3 0.3 convolution_add_fusion.2
  48.6 0.7 dynamic_slice.34
  50.0 4.1 %fusion.70 = (f32[512,512]{1,0:T(8,128)S(1)}, f32[512,512]{1,0:T(8,128)S(1)}) fusion(s32[512]{0:T(512)S(1)} %get-tuple-element.138, s32[512]{0:T(512)S(1)} %get-tuple-element.139), kind=kLoop, calls=%fused_computation.16.clone.1 | loop fusion | flops 3670016 | bytes 2101248 | tf_op jit(solution)/shard_map/while/body/eval_jaxpr/cos | solution.py:17
  54.1 0.3 fusion.71
  54.4 0.3 convolution_add_fusion.2
  54.7 0.7 dynamic_slice.34
  56.1 4.1 %fusion.70 = (f32[512,512]{1,0:T(8,128)S(1)}, f32[512,512]{1,0:T(8,128)S(1)}) fusion(s32[512]{0:T(512)S(1)} %get-tuple-element.138, s32[512]{0:T(512)S(1)} %get-tuple-element.139), kind=kLoop, calls=%fused_computation.16.clone.1 | loop fusion | flops 3670016 | bytes 2101248 | tf_op jit(solution)/shard_map/while/body/eval_jaxpr/cos | solution.py:17
  60.2 0.3 fusion.71
  60.5 0.3 convolution_add_fusion.2
  60.8 0.7 dynamic_slice.34
  62.2 4.1 %fusion.70 = (f32[512,512]{1,0:T(8,128)S(1)}, f32[512,512]{1,0:T(8,128)S(1)}) fusion(s32[512]{0:T(512)S(1)} %get-tuple-element.138, s32[512]{0:T(512)S(1)} %get-tuple-element.139), kind=kLoop, calls=%fused_computation.16.clone.1 | loop fusion | flops 3670016 | bytes 2101248 | tf_op jit(solution)/shard_map/while/body/eval_jaxpr/cos | solution.py:17
  66.4 0.3 fusion.71
  66.6 0.3 convolution_add_fusion.2
  66.9 0.4 add_reduce_fusion
  67.4 0.6 compare_select_fusion
  68.1 31.6 %all_gather.3 = bf16[8,32,2,512]{3,1,0,2:T(8,128)(2,1)S(1)} all-gather(bf16[1,32,2,512]{3,1,0,2:T(8,128)(2,1)S(1)} %pad_maximum_fusion.1), channel_id=1, replica_groups=mesh['pair'=8,'row'=4] {'pair'}, dimensions={0}, use_global_device_ids=true | all-gather | bytes 589824 | tf_op jit(solution)/shard_map/all_gather | solution.py:91
  99.9 2.3 %fusion.28 = f32[2,8,32,256]{3,2,1,0:T(8,128)S(1)} fusion(bf16[1,8,32,512]{3,2,1,0:T(8,128)(2,1)S(1)} %get-tuple-element.99, bf16[1,8,32,512]{3,2,1,0:T(8,128)(2,1)S(1)} %get-tuple-element.98, s32[256]{0:T(256)S(1)} %iota_add_fusion.3, s32[512]{0:T(512)S(1)} %iota_add_fusion.2, f32[512]{0:T(512)S(1)} %multiply_multiply_fusion), kind=kOutput, calls=%fused_computation.45 | convolution fusion | flops 136577024 | bytes 1053696 | tf_op jit(solution)/shard_map/dot_general | solution.py:38
  102.6 35.2 %all-reduce = (f32[32,8,8]{0,1,2:T(8,128)S(1)}, f32[32,8]{0,1:T(8,128)S(1)}) all-reduce(f32[32,8,8]{0,1,2:T(8,128)S(1)} %multiply_subtract_fusion, f32[32,8]{0,1:T(8,128)S(1)} %get-tuple-element.104), channel_id=1, replica_groups=mesh['pair'=8,'row'=4] {'pair'}, use_global_device_ids=true, to_apply=%region_5.6 | all-reduce | flops 2304 | bytes 18432 | tf_op jit(solution)/shard_map/psum | solution.py:105
  137.8 0.6 gather_fusion
  138.4 0.7 reduce_sum.57
  139.7 6.3 %psum.22 = f32[]{:T(128)} all-reduce(f32[]{:T(128)} %reduce_sum.57), channel_id=1, replica_groups=mesh['pair'=8,'row'=4] {'row'}, use_global_device_ids=true, to_apply=%region_7.8 | all-reduce | flops 1 | bytes 8 | tf_op jit(solution)/shard_map/psum | solution.py:107
  146.9 23.5 %custom-call.11 = f32[32,8,8]{2,1,0:T(8,128)S(1)} custom-call(f32[32,8,8]{2,1,0:T(8,128)S(1)} %broadcast_multiply_fusion), custom_call_target="Cholesky" | custom-call | tf_op jit(solution)/shard_map/jit(cholesky)/cholesky | solution.py:111
  170.7 0.7 custom-call.12
  171.5 0.5 dynamic-slice_bitcast_fusion
  (45 shorter events, 1.5 us)
Async XLA Ops:
  0.0 9.2 %copy-start.1 = (s32[8]{0:T(128)S(1)}, s32[8]{0:T(128)}, u32[]{:S(2)}) copy-start(s32[8]{0:T(128)} %param.8) | copy-start | bytes 100
  1.7 16.2 %all-to-all-start = ((bf16[32,512,8]{1,0,2:T(8,128)(2,1)}), bf16[32,512,8]{1,0,2:T(8,128)(2,1)S(1)}, u32[]{:S(2)}, u32[]{:S(2)}) async-start(bf16[32,512,8]{1,0,2:T(8,128)(2,1)} %copy.35), calls=%async_computation | async-start | bytes 524288 | tf_op jit(solution)/shard_map/all_to_all | solution.py:48
  18.0 49.0 %copy-start = (f32[1,32]{1,0:T(1,128)S(1)}, f32[1,32]{1,0:T(1,128)}, u32[]{:S(2)}) copy-start(f32[1,32]{1,0:T(1,128)} %param.7) | copy-start | bytes 388
where the time goes:
time: 172 us
  blocking collectives  73.1 us (42%)
  other arithmetic  60.2 us (35%)
  local copies, waits for them, and re-layouts  9.21 us (5%)
  waiting for transfers between devices  8.06 us (5%)
  starting transfers between devices  7.28 us (4%)
  matrix products  6.83 us (4%)
  loops' own time  5.79 us (3%)
    psum x1, blocking collectives, per_device(): hessian, gradient = lax.psum((hessian, gradient), 'pair')  35.2 us
    cos x8, other arithmetic, band_table(): return jnp.concatenate([jnp.cos(angles), jnp.sin(angles)], axis=1)  33.2 us
    all_gather x1, blocking collectives, per_device(): segment = lax.all_gather(own_spec[None], 'pair', axis=0, tiled=True)  31.6 us
    another operation x4, other arithmetic, per_device(): factor = jnp.linalg.cholesky(system)  23.6 us
    all_to_all x1, waiting for transfers between devices, per_device(): lax.all_to_all(records, 'pair', split_axis=2, concat_axis=1, tiled=True)  8.06 us
    all_to_all x1, starting transfers between devices, per_device(): lax.all_to_all(records, 'pair', split_axis=2, concat_axis=1, tiled=True)  7.28 us
    psum x1, blocking collectives, per_device(): trace_sum = lax.psum(jnp.sum(diagonal), 'row')  6.25 us
    another operation x1, loops' own time, per_device(): lax.scan(accumulate, jnp.zeros((channels, 2 * NF), jnp.float32), jnp.aran...  5.79 us
  transfers between devices with their start and end apart: 1, of which 1 were waited for; matrix products, arithmetic and copies ran while one was open for 0% of the time, Pallas kernels for 0%

commit v1 on v0

--- a/solution.py
+++ b/solution.py
@@ -45,7 +45,10 @@
     nblock = lax.axis_size("pair")
     block_rank = lax.axis_index("pair")
     quarter = lax.axis_index("row")
-    relaid = lax.all_to_all(records, "pair", split_axis=2, concat_axis=1, tiled=True)
+    relaid = jnp.concatenate(
+        lax.all_to_all(jnp.stack(jnp.split(records, lax.axis_size("pair"), axis=2)), "pair", 0, 0),
+        axis=1,
+    )
     signal = relaid[:, :, 0]
     channels = signal.shape[0]
     samples = signal.shape[1]

time: 172 us -> 178 us (1.035)
  local copies, waits for them, and re-layouts: 9.21 us -> 15.1 us
    split x0 -> x1, local copies, waits for them, and re-layouts: none -> 2.73 us  [per_device(): jnp.split(records, lax.axis_size('pair'), axis=2)]
    unnamed x6 -> x12, local copies, waits for them, and re-layouts: 1.77 us -> 4.29 us
where the time goes in v1:
time: 178 us
  blocking collectives  73 us (41%)
  other arithmetic  60.2 us (34%)
  local copies, waits for them, and re-layouts  15.1 us (8%)
  waiting for transfers between devices  8.06 us (5%)
  starting transfers between devices  7.28 us (4%)
  matrix products  6.85 us (4%)
  loops' own time  5.76 us (3%)
    psum x1, blocking collectives, per_device(): hessian, gradient = lax.psum((hessian, gradient), 'pair')  35.2 us
    cos x8, other arithmetic, band_table(): return jnp.concatenate([jnp.cos(angles), jnp.sin(angles)], axis=1)  33.2 us
    all_gather x1, blocking collectives, per_device(): segment = lax.all_gather(own_spec[None], 'pair', axis=0, tiled=True)  31.6 us
    another operation x4, other arithmetic, per_device(): factor = jnp.linalg.cholesky(system)  23.6 us
    all_to_all x1, waiting for transfers between devices, per_device(): lax.all_to_all(jnp.stack(jnp.split(records, lax.axis_size('pair'), axis=2...  8.06 us
    all_to_all x1, starting transfers between devices, per_device(): lax.all_to_all(jnp.stack(jnp.split(records, lax.axis_size('pair'), axis=2...  7.28 us
    psum x1, blocking collectives, per_device(): trace_sum = lax.psum(jnp.sum(diagonal), 'row')  6.25 us
    another operation x1, loops' own time, per_device(): lax.scan(accumulate, jnp.zeros((channels, 2 * NF), jnp.float32), jnp.aran...  5.76 us
  transfers between devices with their start and end apart: 1, of which 1 were waited for; matrix products, arithmetic and copies ran while one was open for 0% of the time, Pallas kernels for 0%

profile of v1, /device:TPU:0, one launch (start us, length us, event | category | flops | bytes accessed | tf_op | source)
XLA Modules:
  0.0 177.8 jit_solution(12998180513503064285)
XLA Ops:
  0.0 2.7 %fusion.70 = (bf16[32,512,1]{1,2,0:T(2,128)(2,1)S(1)}, bf16[32,512,1]{1,2,0:T(2,128)(2,1)S(1)}, bf16[32,512,1]{1,2,0:T(2,128)(2,1)S(1)}, bf16[32,512,1]{1,2,0:T(...) fusion(bf16[32,512,8]{1,2,0:T(8,128)(2,1)} %param.6), kind=kLoop, calls=%fused_computation.128 | loop fusion | bytes 524288 | tf_op jit(solution)/shard_map/split | solution.py:49
  2.7 0.6 fusion.55
  3.4 0.6 fusion.54
  4.0 0.6 fusion.53
  4.6 0.6 fusion.52
  5.2 0.6 fusion.51
  5.8 0.6 fusion.50
  6.4 0.6 fusion.49
  7.0 0.6 fusion.48
  7.6 7.3 %all-to-all-start = ((bf16[8,32,512,1]{2,1,3,0:T(8,128)(2,1)}), bf16[8,32,512,1]{2,1,3,0:T(8,128)(2,1)S(1)}, u32[]{:S(2)}, u32[]{:S(2)}) async-start(bf16[8,32,512,1]{2,1,3,0:T(8,128)(2,1)} %fusion.48), calls=%async_computation | async-start | bytes 524288 | tf_op jit(solution)/shard_map/all_to_all | solution.py:49
  15.0 0.6 dynamic_slice.20
  15.8 8.1 %all-to-all-done = bf16[8,32,512,1]{2,1,3,0:T(8,128)(2,1)S(1)} async-done(((bf16[8,32,512,1]{2,1,3,0:T(8,128)(2,1)}), bf16[8,32,512,1]{2,1,3,0:T(8,128)(2,1)S(1)}, u32[]{:S(2)}, u32[]{:S(2)}) %all-to-all-start) | async-done | bytes 262176 | tf_op jit(solution)/shard_map/all_to_all | solution.py:49
  23.9 48.9 %while.13 = (s32[]{:T(128)}, f32[32,1024]{1,0:T(8,128)S(1)}, s32[8]{0:T(128)S(1)}, bf16[32,4096]{1,0:T(8,128)(2,1)S(1)}, s32[]{:T(128)}, /*index=5*/s32[1]{0:T(128)}, s32[]{:T(128)}, s32[]{:T(128)}) while((s32[]{:T(128)}, f32[32,1024]{1,0:T(8,128)S(1)}, s32[8]{0:T(128)S(1)}, bf16[32,4096]{1,0:T(8,128)(2,1)S(1)}, s32[]{:T(128)}, ...), condition=%wide.region_1.2_spmd.clone, body=%wide.region_0.1_spmd.clone.sunk | while | flops 75596808 | bytes 6889637 | solution.py:72
  23.9 0.7 dynamic_slice.34
  25.3 4.1 %fusion.79 = (f32[512,512]{1,0:T(8,128)S(1)}, f32[512,512]{1,0:T(8,128)S(1)}) fusion(s32[512]{0:T(512)S(1)} %get-tuple-element.146, s32[512]{0:T(512)S(1)} %get-tuple-element.147), kind=kLoop, calls=%fused_computation.16.clone.1 | loop fusion | flops 3670016 | bytes 2101248 | tf_op jit(solution)/shard_map/while/body/eval_jaxpr/cos | solution.py:17
  29.4 0.3 fusion.80
  30.0 0.7 dynamic_slice.34
  31.4 4.1 %fusion.79 = (f32[512,512]{1,0:T(8,128)S(1)}, f32[512,512]{1,0:T(8,128)S(1)}) fusion(s32[512]{0:T(512)S(1)} %get-tuple-element.146, s32[512]{0:T(512)S(1)} %get-tuple-element.147), kind=kLoop, calls=%fused_computation.16.clone.1 | loop fusion | flops 3670016 | bytes 2101248 | tf_op jit(solution)/shard_map/while/body/eval_jaxpr/cos | solution.py:17
  35.5 0.3 fusion.80
  36.1 0.7 dynamic_slice.34
  37.5 4.1 %fusion.79 = (f32[512,512]{1,0:T(8,128)S(1)}, f32[512,512]{1,0:T(8,128)S(1)}) fusion(s32[512]{0:T(512)S(1)} %get-tuple-element.146, s32[512]{0:T(512)S(1)} %get-tuple-element.147), kind=kLoop, calls=%fused_computation.16.clone.1 | loop fusion | flops 3670016 | bytes 2101248 | tf_op jit(solution)/shard_map/while/body/eval_jaxpr/cos | solution.py:17
  41.6 0.3 fusion.80
  42.2 0.7 dynamic_slice.34
  43.6 4.1 %fusion.79 = (f32[512,512]{1,0:T(8,128)S(1)}, f32[512,512]{1,0:T(8,128)S(1)}) fusion(s32[512]{0:T(512)S(1)} %get-tuple-element.146, s32[512]{0:T(512)S(1)} %get-tuple-element.147), kind=kLoop, calls=%fused_computation.16.clone.1 | loop fusion | flops 3670016 | bytes 2101248 | tf_op jit(solution)/shard_map/while/body/eval_jaxpr/cos | solution.py:17
  47.8 0.3 fusion.80
  48.3 0.7 dynamic_slice.34
  49.7 4.1 %fusion.79 = (f32[512,512]{1,0:T(8,128)S(1)}, f32[512,512]{1,0:T(8,128)S(1)}) fusion(s32[512]{0:T(512)S(1)} %get-tuple-element.146, s32[512]{0:T(512)S(1)} %get-tuple-element.147), kind=kLoop, calls=%fused_computation.16.clone.1 | loop fusion | flops 3670016 | bytes 2101248 | tf_op jit(solution)/shard_map/while/body/eval_jaxpr/cos | solution.py:17
  53.9 0.3 fusion.80
  54.4 0.7 dynamic_slice.34
  55.8 4.1 %fusion.79 = (f32[512,512]{1,0:T(8,128)S(1)}, f32[512,512]{1,0:T(8,128)S(1)}) fusion(s32[512]{0:T(512)S(1)} %get-tuple-element.146, s32[512]{0:T(512)S(1)} %get-tuple-element.147), kind=kLoop, calls=%fused_computation.16.clone.1 | loop fusion | flops 3670016 | bytes 2101248 | tf_op jit(solution)/shard_map/while/body/eval_jaxpr/cos | solution.py:17
  60.0 0.3 fusion.80
  60.6 0.7 dynamic_slice.34
  61.9 4.1 %fusion.79 = (f32[512,512]{1,0:T(8,128)S(1)}, f32[512,512]{1,0:T(8,128)S(1)}) fusion(s32[512]{0:T(512)S(1)} %get-tuple-element.146, s32[512]{0:T(512)S(1)} %get-tuple-element.147), kind=kLoop, calls=%fused_computation.16.clone.1 | loop fusion | flops 3670016 | bytes 2101248 | tf_op jit(solution)/shard_map/while/body/eval_jaxpr/cos | solution.py:17
  66.1 0.3 fusion.80
  66.7 0.7 dynamic_slice.34
  68.1 4.1 %fusion.79 = (f32[512,512]{1,0:T(8,128)S(1)}, f32[512,512]{1,0:T(8,128)S(1)}) fusion(s32[512]{0:T(512)S(1)} %get-tuple-element.146, s32[512]{0:T(512)S(1)} %get-tuple-element.147), kind=kLoop, calls=%fused_computation.16.clone.1 | loop fusion | flops 3670016 | bytes 2101248 | tf_op jit(solution)/shard_map/while/body/eval_jaxpr/cos | solution.py:17
  72.2 0.3 fusion.80
  72.8 0.4 add_reduce_fusion
  73.2 0.6 compare_select_fusion
  74.0 31.6 %all_gather.3 = bf16[8,32,2,512]{3,1,0,2:T(8,128)(2,1)S(1)} all-gather(bf16[1,32,2,512]{3,1,0,2:T(8,128)(2,1)S(1)} %pad_maximum_fusion.1), channel_id=1, replica_groups=mesh['pair'=8,'row'=4] {'pair'}, dimensions={0}, use_global_device_ids=true | all-gather | bytes 589824 | tf_op jit(solution)/shard_map/all_gather | solution.py:94
  105.7 2.3 %fusion.28 = f32[2,8,32,256]{3,2,1,0:T(8,128)S(1)} fusion(bf16[1,8,32,512]{3,2,1,0:T(8,128)(2,1)S(1)} %get-tuple-element.99, bf16[1,8,32,512]{3,2,1,0:T(8,128)(2,1)S(1)} %get-tuple-element.98, s32[256]{0:T(256)S(1)} %iota_add_fusion.3, s32[512]{0:T(512)S(1)} %iota_add_fusion.2, f32[512]{0:T(512)S(1)} %multiply_multiply_fusion), kind=kOutput, calls=%fused_computation.45 | convolution fusion | flops 136577024 | bytes 1053696 | tf_op jit(solution)/shard_map/dot_general | solution.py:38
  108.4 35.2 %all-reduce = (f32[32,8,8]{0,1,2:T(8,128)S(1)}, f32[32,8]{0,1:T(8,128)S(1)}) all-reduce(f32[32,8,8]{0,1,2:T(8,128)S(1)} %multiply_subtract_fusion, f32[32,8]{0,1:T(8,128)S(1)} %get-tuple-element.112), channel_id=1, replica_groups=mesh['pair'=8,'row'=4] {'pair'}, use_global_device_ids=true, to_apply=%region_5.6 | all-reduce | flops 2304 | bytes 18432 | tf_op jit(solution)/shard_map/psum | solution.py:108
  143.7 0.6 gather_fusion
  144.2 0.7 reduce_sum.57
  145.6 6.3 %psum.22 = f32[]{:T(128)} all-reduce(f32[]{:T(128)} %reduce_sum.57), channel_id=1, replica_groups=mesh['pair'=8,'row'=4] {'row'}, use_global_device_ids=true, to_apply=%region_7.8 | all-reduce | flops 1 | bytes 8 | tf_op jit(solution)/shard_map/psum | solution.py:110
  152.8 23.5 %custom-call.11 = f32[32,8,8]{2,1,0:T(8,128)S(1)} custom-call(f32[32,8,8]{2,1,0:T(8,128)S(1)} %broadcast_multiply_fusion), custom_call_target="Cholesky" | custom-call | tf_op jit(solution)/shard_map/jit(cholesky)/cholesky | solution.py:114
  176.6 0.7 custom-call.12
  177.3 0.5 dynamic-slice_bitcast_fusion
  (53 shorter events, 3.8 us)
Async XLA Ops:
  0.0 15.0 %copy-start.1 = (s32[8]{0:T(128)S(1)}, s32[8]{0:T(128)}, u32[]{:S(2)}) copy-start(s32[8]{0:T(128)} %param.8) | copy-start | bytes 100
  7.6 16.2 %all-to-all-start = ((bf16[8,32,512,1]{2,1,3,0:T(8,128)(2,1)}), bf16[8,32,512,1]{2,1,3,0:T(8,128)(2,1)S(1)}, u32[]{:S(2)}, u32[]{:S(2)}) async-start(bf16[8,32,512,1]{2,1,3,0:T(8,128)(2,1)} %fusion.48), calls=%async_computation | async-start | bytes 524288 | tf_op jit(solution)/shard_map/all_to_all | solution.py:49
  23.9 48.9 %copy-start = (f32[1,32]{1,0:T(1,128)S(1)}, f32[1,32]{1,0:T(1,128)}, u32[]{:S(2)}) copy-start(f32[1,32]{1,0:T(1,128)} %param.7) | copy-start | bytes 388
